TPU v7x, 256 devices: a whole 4x4x8 slice. The times are simulated.
256 devices in a mesh: row: 8 (over x, z_hi), col: 8 (over z_lo, core), layer: 4 (over y).
Axes of the slice: x: 4, y: 4, z: 8 (z_hi: 2, z_lo: 4; z = z_hi * 4 + z_lo), core: 2. Of those that a mesh axis runs over, the one named last changes fastest.
Arguments:
- amplitudes: float32 [4096, 2048], P('row', ('col', 'layer')), may hold values from -6 to 6
- integrals: float32 [2048, 16384], P(('row', 'layer'), 'col'), may hold values from -0.125 to 0.125
Outputs:
- ladder: float32 [4096, 16384], P('row', ('col', 'layer'))
All inputs are finite; a program needn't handle non-finite values.
Results may differ from a plain program's by a relative error of at most 0.000082.
Values sent between devices are 32-bit elements; how exact they have to be, the bound alone decides.
A program may use at most 64 MiB of HBM per device.

v0:
```python
import jax
import jax.numpy as jnp
from jax import lax
from jax.sharding import PartitionSpec as P


def from_root(block, axis, holder):
    block = jnp.where(lax.axis_index(axis) == holder, block, jnp.zeros_like(block))
    return lax.psum(block, axis)


def summa(amp_panel, int_panel, step_count, first_step):
    spread = lax.axis_size("col") // lax.axis_size("row")
    partial_sum = jnp.zeros((amp_panel.shape[0], int_panel.shape[1]), jnp.float32)

    def one_turn(turn_at, total):
        block_at = first_step + turn_at
        amp_block = from_root(amp_panel, "col", block_at)
        int_block = from_root(int_panel, "row", block_at // spread)
        return total + jnp.dot(
            amp_block,
            int_block,
            precision=lax.Precision.HIGHEST,
            preferred_element_type=jnp.float32,
        )

    return lax.fori_loop(0, step_count, one_turn, partial_sum)


def contract(amp_panel, int_panel, step_count, first_step):
    return summa(amp_panel, int_panel, step_count, first_step)


def shards(amplitudes, integrals):
    cols_n = lax.axis_size("col")
    layers_n = lax.axis_size("layer")
    layer_at = lax.axis_index("layer")
    amp_panel = lax.all_gather(amplitudes, "layer", axis=1, tiled=True)
    int_panel = lax.all_gather(integrals, "layer", axis=0, tiled=True)
    step_count = cols_n // layers_n
    partial_sum = contract(amp_panel, int_panel, step_count, layer_at * step_count)
    product = lax.psum_scatter(partial_sum, "layer", scatter_dimension=1, tiled=True)
    return 0.5 * product


def solution(mesh):
    in_specs = (P("row", ("col", "layer")), P(("row", "layer"), "col"))
    out_specs = P("row", ("col", "layer"))
    return jax.shard_map(shards, mesh=mesh, in_specs=in_specs, out_specs=out_specs, check_vma=False)
```

profile of v0, /device:TPU:1, one launch (start us, length us, event | category | flops | bytes accessed | tf_op | source)
XLA Modules:
  0.0 660.9 jit_solution(806559248901591180)
XLA Ops:
  6.5 0.0 all-gather.2.cloned.1.call-start
  6.5 0.7 all-gather.2.cloned.1.call-update
  7.3 12.8 %all_gather.6 = f32[512,256]{0,1:T(8,128)S(1)} all-gather(f32[512,64]{0,1:T(8,128)} %param.4), channel_id=1, replica_groups=mesh['row'=8,'col'=8,'layer'=4] {'layer'}, dimensions={1}, use_global_device_ids=true | all-gather | bytes 655360 | tf_op jit(solution)/shard_map/all_gather | solution.py:38
  20.1 0.2 copy.4
  20.3 25.9 %all-gather.2.cloned.1.call-done = f32[256,2048]{1,0:T(8,128)} async-done(((f32[64,2048]{1,0:T(8,128)}), f32[256,2048]{1,0:T(8,128)}) %all-gather.2.cloned.1.call-update) | async-done | bytes 2097168 | tf_op jit(solution)/shard_map/all_gather | solution.py:39
  46.1 555.9 %while.16 = (s32[]{:T(128)}, f32[512,2048]{1,0:T(8,128)}, s32[]{:T(128)}, f32[512,256]{1,0:T(8,128)S(1)}, f32[256,2048]{1,0:T(8,128)}, /*index=5*/s32[]{:T(128)}, u32[]{:T(128)}, u32[]{:T(128)}, u32[]{:T(128)}, s32[]{:T(128)}) while((s32[]{:T(128)}, f32[512,2048]{1,0:T(8,128)}, s32[]{:T(128)}, f32[512,256]{1,0:T(8,128)S(1)}, ...), condition=%wide.region_3.4_spmd.clone, body=%wide.region_0.3_spmd.clone.sunk | while | flops 3224633344 | bytes 31981860 | solution.py:27
  46.1 0.0 all-reduce.3.cloned.1.call-start
  46.1 0.8 broadcast_select_fusion.4
  47.0 0.0 all-reduce.3.cloned.1.call-update
  47.0 0.0 all-reduce.5.cloned.1.call-start
  47.1 3.2 broadcast_select_fusion.5
  50.2 0.0 all-reduce.5.cloned.1.call-update
  50.3 68.8 %all-reduce.3.cloned.1.call-done = f32[512,256]{1,0:T(8,128)} async-done(((f32[512,256]{1,0:T(8,128)}), f32[512,256]{1,0:T(8,128)}) %all-reduce.3.cloned.1.call-update) | async-done | bytes 524304 | tf_op jit(solution)/shard_map/while/body/eval_jaxpr/psum | solution.py:9
  119.1 198.7 %all-reduce.5.cloned.1.call-done = f32[256,2048]{1,0:T(8,128)} async-done(((f32[256,2048]{1,0:T(8,128)}), f32[256,2048]{1,0:T(8,128)}) %all-reduce.5.cloned.1.call-update) | async-done | bytes 2097168 | tf_op jit(solution)/shard_map/while/body/eval_jaxpr/psum | solution.py:9
  317.8 7.4 %select_add_fusion.2 = f32[512,2048]{1,0:T(8,128)} fusion(f32[512,2048]{1,0:T(8,128)} %get-tuple-element.215, f32[512,256]{1,0:T(8,128)} %all-reduce.3.cloned.1.call-done, f32[256,2048]{1,0:T(8,128)} %all-reduce.5.cloned.1.call-done, pred[]{:T(512)S(6)} %compare.9), kind=kOutput, calls=%fused_computation.clone.1 | convolution fusion | flops 3223322624 | bytes 11010049 | tf_op jit(solution)/shard_map/while/body/eval_jaxpr/dot_general | solution.py:20
  325.2 0.0 all-reduce.3.cloned.1.call-start
  325.2 0.8 broadcast_select_fusion.4
  326.0 0.0 all-reduce.3.cloned.1.call-update
  326.0 0.0 all-reduce.5.cloned.1.call-start
  326.1 1.6 broadcast_select_fusion.5
  327.6 0.0 all-reduce.5.cloned.1.call-update
  327.7 67.2 %all-reduce.3.cloned.1.call-done = f32[512,256]{1,0:T(8,128)} async-done(((f32[512,256]{1,0:T(8,128)}), f32[512,256]{1,0:T(8,128)}) %all-reduce.3.cloned.1.call-update) | async-done | bytes 524304 | tf_op jit(solution)/shard_map/while/body/eval_jaxpr/psum | solution.py:9
  394.8 198.5 %all-reduce.5.cloned.1.call-done = f32[256,2048]{1,0:T(8,128)} async-done(((f32[256,2048]{1,0:T(8,128)}), f32[256,2048]{1,0:T(8,128)}) %all-reduce.5.cloned.1.call-update) | async-done | bytes 2097168 | tf_op jit(solution)/shard_map/while/body/eval_jaxpr/psum | solution.py:9
  593.4 8.6 %select_add_fusion.2 = f32[512,2048]{1,0:T(8,128)} fusion(f32[512,2048]{1,0:T(8,128)} %get-tuple-element.215, f32[512,256]{1,0:T(8,128)} %all-reduce.3.cloned.1.call-done, f32[256,2048]{1,0:T(8,128)} %all-reduce.5.cloned.1.call-done, pred[]{:T(512)S(6)} %compare.9), kind=kOutput, calls=%fused_computation.clone.1 | convolution fusion | flops 3223322624 | bytes 11010049 | tf_op jit(solution)/shard_map/while/body/eval_jaxpr/dot_general | solution.py:20
  602.0 0.0 reduce-scatter.2.cloned.1.call-start
  602.0 0.6 reduce-scatter.2.cloned.1.call-update
  602.6 49.1 %reduce-scatter.2.cloned.1.call-done = f32[512,512]{1,0:T(8,128)} async-done(((f32[512,2048]{1,0:T(8,128)}), f32[512,512]{1,0:T(8,128)}) %reduce-scatter.2.cloned.1.call-update) | async-done | bytes 1048592 | tf_op jit(solution)/shard_map/reduce_scatter | solution.py:42
  651.7 2.3 broadcast_multiply_fusion
  (1 shorter events, 0.0 us)
Async XLA Ops:
  6.5 39.6 %all-gather.2.cloned.1.call-start = ((), (), s32[]{:S(2)}) async-start(), calls=%async_computation.1 | async-start | bytes 2621440 | tf_op jit(solution)/shard_map/all_gather | solution.py:39
  46.1 72.9 %all-reduce.3.cloned.1.call-start = ((), (), s32[]{:S(2)}) async-start(), calls=%async_computation.3 | async-start | bytes 1048576 | tf_op jit(solution)/shard_map/while/body/eval_jaxpr/psum | solution.py:9
  47.0 270.8 %all-reduce.5.cloned.1.call-start = ((), (), s32[]{:S(2)}) async-start(), calls=%async_computation.4 | async-start | bytes 4194304 | tf_op jit(solution)/shard_map/while/body/eval_jaxpr/psum | solution.py:9
  325.2 69.7 %all-reduce.3.cloned.1.call-start = ((), (), s32[]{:S(2)}) async-start(), calls=%async_computation.3 | async-start | bytes 1048576 | tf_op jit(solution)/shard_map/while/body/eval_jaxpr/psum | solution.py:9
  326.0 267.4 %all-reduce.5.cloned.1.call-start = ((), (), s32[]{:S(2)}) async-start(), calls=%async_computation.4 | async-start | bytes 4194304 | tf_op jit(solution)/shard_map/while/body/eval_jaxpr/psum | solution.py:9
  602.0 49.7 %reduce-scatter.2.cloned.1.call-start = ((), (), s32[]{:S(2)}) async-start(), calls=%async_computation.2 | async-start | bytes 5242880 | tf_op jit(solution)/shard_map/reduce_scatter | solution.py:42
Sparse Core Ops, SparseCore 0:
  9.1 36.9 all-gather.1
  49.6 69.4 all-reduce.2
  121.7 195.9 all-reduce.4
  328.3 66.5 all-reduce.2
  397.4 195.9 all-reduce.4
  605.0 46.6 reduce-scatter.1
where the time goes:
time: 661 us
  waiting for transfers between devices  610 us (92%)
  matrix products  16 us (2%)
  between operations  13.4 us (2%)
  blocking collectives  12.8 us (2%)
  other arithmetic  8.69 us (1%)
    psum x4, waiting for transfers between devices, from_root(): return lax.psum(block, axis)  533 us
    reduce_scatter x1, waiting for transfers between devices, shards(): lax.psum_scatter(partial_sum, 'layer', scatter_dimension=1, tiled=True)  49.1 us
    all_gather x1, waiting for transfers between devices, shards(): int_panel = lax.all_gather(integrals, 'layer', axis=0, tiled=True)  25.9 us
    dot_general x2, matrix products, one_turn(): jnp.dot(amp_block, int_block, precision=lax.Precision.HIGHEST, preferred_...  16 us
  transfers between devices with their start and end apart: 6, of which 6 were waited for; matrix products, arithmetic and copies ran while one was open for 1% of the time, Pallas kernels for 0%

commit v1 on v0

--- a/solution.py
+++ b/solution.py
@@ -6,7 +6,7 @@
 
 def from_root(block, axis, holder):
     block = jnp.where(lax.axis_index(axis) == holder, block, jnp.zeros_like(block))
-    return lax.psum(block, axis)
+    return jnp.sum(lax.all_gather(block, axis), axis=0)
 
 
 def summa(amp_panel, int_panel, step_count, first_step):

time: 661 us -> 855 us (1.29)
  waiting for transfers between devices: 610 us -> 787 us
  other arithmetic: 8.69 us -> 29.2 us
    all_gather x0 -> x4, waiting for transfers between devices: none -> 712 us  [from_root(): return jnp.sum(lax.all_gather(block, axis), axis=0)]
    psum x4 -> x0, waiting for transfers between devices: 533 us -> none  [from_root(): return lax.psum(block, axis)]
    reduce_sum x0 -> x4, other arithmetic: none -> 20.6 us  [from_root(): return jnp.sum(lax.all_gather(block, axis), axis=0)]
where the time goes in v1:
time: 855 us
  waiting for transfers between devices  787 us (92%)
  other arithmetic  29.2 us (3%)
  between operations  13.4 us (2%)
  blocking collectives  12.8 us (1%)
  matrix products  12.2 us (1%)
    all_gather x4, waiting for transfers between devices, from_root(): return jnp.sum(lax.all_gather(block, axis), axis=0)  712 us
    reduce_scatter x1, waiting for transfers between devices, shards(): lax.psum_scatter(partial_sum, 'layer', scatter_dimension=1, tiled=True)  47.2 us
    all_gather x1, waiting for transfers between devices, shards(): int_panel = lax.all_gather(integrals, 'layer', axis=0, tiled=True)  25.9 us
    reduce_sum x4, other arithmetic, from_root(): return jnp.sum(lax.all_gather(block, axis), axis=0)  20.6 us
  transfers between devices with their start and end apart: 6, of which 6 were waited for; matrix products, arithmetic and copies ran while one was open for 1% of the time, Pallas kernels for 0%

profile of v1, /device:TPU:1, one launch (start us, length us, event | category | flops | bytes accessed | tf_op | source)
XLA Modules:
  0.0 854.8 jit_solution(3856589927848293111)
XLA Ops:
  6.5 0.0 all-gather.12.cloned.1.call-start
  6.5 0.7 all-gather.12.cloned.1.call-update
  7.3 12.8 %all_gather.32 = f32[512,256]{0,1:T(8,128)S(1)} all-gather(f32[512,64]{0,1:T(8,128)} %param.4), channel_id=1, replica_groups=mesh['row'=8,'col'=8,'layer'=4] {'layer'}, dimensions={1}, use_global_device_ids=true | all-gather | bytes 655360 | tf_op jit(solution)/shard_map/all_gather | solution.py:38
  20.1 0.2 copy.4
  20.3 25.9 %all-gather.12.cloned.1.call-done = f32[256,2048]{1,0:T(8,128)} async-done(((f32[64,2048]{1,0:T(8,128)}), f32[256,2048]{1,0:T(8,128)}) %all-gather.12.cloned.1.call-update) | async-done | bytes 2097168 | tf_op jit(solution)/shard_map/all_gather | solution.py:39
  46.1 751.7 %while.16 = (s32[]{:T(128)}, f32[512,2048]{1,0:T(8,128)}, s32[]{:T(128)}, f32[512,256]{1,0:T(8,128)S(1)}, f32[256,2048]{1,0:T(8,128)}, /*index=5*/s32[]{:T(128)}...) while((s32[]{:T(128)}, f32[512,2048]{1,0:T(8,128)}, s32[]{:T(128)}, ...), condition=%wide.region_3.4_spmd.clone, body=%wide.region_0.3_spmd.clone.sunk | while | flops 3228565504 | bytes 110625064 | solution.py:27
  46.1 0.0 all-gather.14.cloned.1.call-start
  46.1 0.8 broadcast_select_fusion.4
  47.0 0.0 all-gather.14.cloned.1.call-update
  47.0 0.0 all-gather.16.cloned.1.call-start
  47.1 3.1 broadcast_select_fusion.5
  50.2 0.0 all-gather.16.cloned.1.call-update
  50.2 51.2 %all-gather.14.cloned.1.call-done = f32[4096,256]{1,0:T(8,128)} async-done(((f32[512,256]{1,0:T(8,128)}), f32[4096,256]{1,0:T(8,128)}) %all-gather.14.cloned.1.call-update) | async-done | bytes 4194320 | tf_op jit(solution)/shard_map/while/body/eval_jaxpr/all_gather | solution.py:9
  101.4 2.5 reduce_sum.36
  103.9 306.9 %all-gather.16.cloned.1.call-done = f32[2048,2048]{1,0:T(8,128)} async-done(((f32[256,2048]{1,0:T(8,128)}), f32[2048,2048]{1,0:T(8,128)}) %all-gather.16.cloned.1.call-update) | async-done | bytes 16777232 | tf_op jit(solution)/shard_map/while/body/eval_jaxpr/all_gather | solution.py:9
  410.8 7.8 reduce_sum.37
  418.6 5.3 select_add_fusion.2
  423.9 0.0 all-gather.14.cloned.1.call-start
  423.9 0.8 broadcast_select_fusion.4
  424.7 0.0 all-gather.14.cloned.1.call-update
  424.8 0.0 all-gather.16.cloned.1.call-start
  424.8 1.5 broadcast_select_fusion.5
  426.3 0.0 all-gather.16.cloned.1.call-update
  426.4 47.6 %all-gather.14.cloned.1.call-done = f32[4096,256]{1,0:T(8,128)} async-done(((f32[512,256]{1,0:T(8,128)}), f32[4096,256]{1,0:T(8,128)}) %all-gather.14.cloned.1.call-update) | async-done | bytes 4194320 | tf_op jit(solution)/shard_map/while/body/eval_jaxpr/all_gather | solution.py:9
  474.0 2.5 reduce_sum.36
  476.5 306.7 %all-gather.16.cloned.1.call-done = f32[2048,2048]{1,0:T(8,128)} async-done(((f32[256,2048]{1,0:T(8,128)}), f32[2048,2048]{1,0:T(8,128)}) %all-gather.16.cloned.1.call-update) | async-done | bytes 16777232 | tf_op jit(solution)/shard_map/while/body/eval_jaxpr/all_gather | solution.py:9
  783.2 7.8 reduce_sum.37
  791.0 6.9 select_add_fusion.2
  797.9 0.0 reduce-scatter.2.cloned.1.call-start
  797.9 0.6 reduce-scatter.2.cloned.1.call-update
  798.5 47.2 %reduce-scatter.2.cloned.1.call-done = f32[512,512]{1,0:T(8,128)} async-done(((f32[512,2048]{1,0:T(8,128)}), f32[512,512]{1,0:T(8,128)}) %reduce-scatter.2.cloned.1.call-update) | async-done | bytes 1048592 | tf_op jit(solution)/shard_map/reduce_scatter | solution.py:42
  845.7 2.3 broadcast_multiply_fusion
  (1 shorter events, 0.0 us)
Async XLA Ops:
  6.5 39.6 %all-gather.12.cloned.1.call-start = ((), (), s32[]{:S(2)}) async-start(), calls=%async_computation.1 | async-start | bytes 2621440 | tf_op jit(solution)/shard_map/all_gather | solution.py:39
  46.1 55.3 %all-gather.14.cloned.1.call-start = ((), (), s32[]{:S(2)}) async-start(), calls=%async_computation.3 | async-start | bytes 4718592 | tf_op jit(solution)/shard_map/while/body/eval_jaxpr/all_gather | solution.py:9
  47.0 363.8 %all-gather.16.cloned.1.call-start = ((), (), s32[]{:S(2)}) async-start(), calls=%async_computation.4 | async-start | bytes 18874368 | tf_op jit(solution)/shard_map/while/body/eval_jaxpr/all_gather | solution.py:9
  423.9 50.1 %all-gather.14.cloned.1.call-start = ((), (), s32[]{:S(2)}) async-start(), calls=%async_computation.3 | async-start | bytes 4718592 | tf_op jit(solution)/shard_map/while/body/eval_jaxpr/all_gather | solution.py:9
  424.8 358.5 %all-gather.16.cloned.1.call-start = ((), (), s32[]{:S(2)}) async-start(), calls=%async_computation.4 | async-start | bytes 18874368 | tf_op jit(solution)/shard_map/while/body/eval_jaxpr/all_gather | solution.py:9
  797.9 47.8 %reduce-scatter.2.cloned.1.call-start = ((), (), s32[]{:S(2)}) async-start(), calls=%async_computation.2 | async-start | bytes 5242880 | tf_op jit(solution)/shard_map/reduce_scatter | solution.py:42
Sparse Core Ops, SparseCore 0:
  9.1 36.9 all-gather.11
  48.7 52.6 all-gather.13
  104.0 306.7 all-gather.15
  426.2 47.8 all-gather.13
  476.5 306.7 all-gather.15
  800.9 44.6 reduce-scatter.1
